TPU v7x, 32 devices: a whole 2x2x4 slice. The times are simulated.
32 devices in a mesh: row: 4 (over z), col: 8 (over y, x, core).
Axes of the slice: x: 2, y: 2, z: 4, core: 2. Of those that a mesh axis runs over, the one named last changes fastest.
Arguments:
- fem_basis: float32 [2, 16, 2, 65536], P(None, None, None, ('row', 'col')), may hold values from -8 to 8
- bem_basis: float32 [2, 16, 2, 16384], P(None, None, None, ('row', 'col')), may hold values from -8 to 8
- fem_diagonal: float32 [65536], P(('row', 'col')), may hold values from 1 to 4
- fem_values: float32 [16, 65536], P(None, ('row', 'col')), may hold values from -1.5 to 1.5
- fem_columns: int32 [16, 65536], P(None, ('row', 'col')), may hold values from 0 to 2559
- halo_rows: int32 [4, 4096], P(None, ('row', 'col')), may hold values from 0 to 2047
- bem_matrix: bfloat16 [2, 16384, 16384], P(None, 'row', 'col'), may hold values from -0.03125 to 0.03125
- trace_rows: int32 [32768], P(('row', 'col')), may hold values from -1 to 2047, as said below
- bem_slot: int32 [16384], P(('row', 'col')), may hold values from 0 to 1023, as said below
Outputs:
- next_fem: float32 [16, 2, 65536], P(None, None, ('row', 'col'))
- next_bem: float32 [16, 2, 16384], P(None, None, ('row', 'col'))
- hessenberg: float32 [2, 16, 16], replicated
- r_factor: float32 [16, 16], replicated
Inputs may be any that keep to these rules, and one draw needn't show every extreme that they name: `trace_rows`: each device's entries form one block of 32 slots per BEM owner, owners in row+col order; a block is all -1 (unused) or holds local FEM rows, the rows of one device being distinct; every owner is fed by exactly 16 full blocks. `bem_slot`: value = source device along row+col times 32 plus slot; within one owner the values are distinct and are exactly the full slots that trace_rows sends to that owner.
All inputs are finite; a program needn't handle non-finite values.
Results may differ from a plain program's by a relative error of at most 0.0014.
Values may be sent and summed in bfloat16 or wider, within the bound.
No kernel may reach another device: no remote copies, remote signals or barrier semaphores. Data moves between devices by JAX's collectives and lax.ppermute only.
A program may use at most 128 MiB of HBM per device.

v0:
```python
import jax
import jax.numpy as jnp
from jax import lax
from jax.sharding import PartitionSpec as P

HIGHEST = lax.Precision.HIGHEST


def with_halo(cells, sides, width):
    for axis, dim in sides:
        count = lax.axis_size(axis)
        ends = count - 1
        head = lax.slice_in_dim(cells, 0, width, axis=dim)
        tail = lax.slice_in_dim(cells, cells.shape[dim] - width, cells.shape[dim], axis=dim)
        cells = jnp.concatenate(
            [
                lax.ppermute(tail, axis, [(i, (i + 1) % count) for i in range(ends)]),
                cells,
                lax.ppermute(head, axis, [((i + 1) % count, i) for i in range(ends)]),
            ],
            axis=dim,
        )
    return cells


def dotted(lefts, rights):
    return lax.dot_general(
        lefts.reshape(lefts.shape[0], -1),
        rights.reshape(rights.shape[0], -1),
        (((1,), (1,)), ((), ())),
        precision=HIGHEST,
        preferred_element_type=jnp.float32,
    )


def combine(coeffs, basis):
    flat_basis = basis.reshape(basis.shape[0], -1)
    merged = lax.dot_general(
        coeffs,
        flat_basis,
        (((0,), (0,)), ((), ())),
        precision=HIGHEST,
        preferred_element_type=jnp.float32,
    )
    return merged.reshape((coeffs.shape[1],) + basis.shape[1:])


def exterior(vectors, halo_rows):
    outbound = jnp.take(vectors, halo_rows, axis=2)
    stacked = outbound.reshape((1, 1, outbound.shape[0] * outbound.shape[1], -1))
    bordered = with_halo(stacked, (("row", 0), ("col", 1)), 1)

    def unpack(cell, direction):
        return cell.reshape(outbound.shape)[:, :, direction]

    from_left = unpack(bordered[1, 0], 0)
    from_right = unpack(bordered[1, 2], 1)
    from_above = unpack(bordered[0, 1], 2)
    from_below = unpack(bordered[2, 1], 3)
    return jnp.concatenate([vectors, from_left, from_right, from_above, from_below], axis=2)


def fem_product(vectors, fem_diagonal, fem_values, fem_columns, halo_rows):
    extended = exterior(vectors, halo_rows)
    gathered = jnp.take(extended, fem_columns, axis=2)
    return fem_diagonal * vectors + jnp.sum(fem_values * gathered, axis=2)


def bem_product(vectors, bem_matrix):
    rounded = vectors.astype(jnp.bfloat16)
    portion = lax.all_gather(rounded, "row", axis=2, tiled=True)
    flat_part = portion.reshape(-1, portion.shape[-1])
    products = lax.dot_general(
        flat_part, bem_matrix, (((1,), (2,)), ((), ())), preferred_element_type=jnp.float32
    )
    products = products.reshape(rounded.shape[0], 2, 2, -1)
    real_part = products[:, 0, 0] - products[:, 1, 1]
    imag_part = products[:, 0, 1] + products[:, 1, 0]
    partial_rows = jnp.stack([real_part, imag_part], axis=1)
    return lax.psum_scatter(partial_rows, "col", scatter_dimension=2, tiled=True)


def body(
    fem_basis,
    bem_basis,
    fem_diagonal,
    fem_values,
    fem_columns,
    halo_rows,
    bem_matrix,
    trace_rows,
    bem_slot,
):
    blocks = fem_basis.shape[0]
    rhs_count = fem_basis.shape[1]
    fem_last = fem_basis[blocks - 1]
    bem_last = bem_basis[blocks - 1]
    fem_image = fem_product(fem_last, fem_diagonal, fem_values, fem_columns, halo_rows)
    bem_image = bem_product(bem_last, bem_matrix)
    active = trace_rows >= 0
    clipped = jnp.where(active, trace_rows, 0)
    mask_row = active.astype(jnp.float32)
    outgoing = jnp.take(fem_last, clipped, axis=2) * mask_row
    slot_count = trace_rows.shape[0]
    selector = (bem_slot[:, None] == jnp.arange(slot_count, dtype=jnp.int32)[None, :]).astype(
        jnp.float32
    )
    returning = lax.dot_general(
        bem_last,
        selector,
        (((2,), (0,)), ((), ())),
        precision=HIGHEST,
        preferred_element_type=jnp.float32,
    )
    arriving, answers = (
        lax.all_to_all(outgoing, ("row", "col"), split_axis=2, concat_axis=2, tiled=True),
        lax.all_to_all(returning, ("row", "col"), split_axis=2, concat_axis=2, tiled=True),
    )
    fem_image = fem_image.at[:, :, clipped].add(answers * mask_row)
    bem_image = bem_image + lax.dot_general(
        arriving,
        selector,
        (((2,), (1,)), ((), ())),
        precision=HIGHEST,
        preferred_element_type=jnp.float32,
    )
    device_count = lax.axis_size("row") * lax.axis_size("col")
    count = 2.0 * device_count * (fem_last.shape[2] + bem_last.shape[2])
    fem_flat = fem_basis.reshape(blocks * rhs_count, 2, -1)
    bem_flat = bem_basis.reshape(blocks * rhs_count, 2, -1)
    coeffs_one = (
        lax.psum(dotted(fem_flat, fem_image) + dotted(bem_flat, bem_image), ("row", "col")) / count
    )
    fem_once = fem_image - combine(coeffs_one, fem_flat)
    bem_once = bem_image - combine(coeffs_one, bem_flat)
    sums_two, gram_once, basis_gram = lax.psum(
        (
            dotted(fem_flat, fem_once) + dotted(bem_flat, bem_once),
            dotted(fem_once, fem_once) + dotted(bem_once, bem_once),
            dotted(fem_flat, fem_flat) + dotted(bem_flat, bem_flat),
        ),
        ("row", "col"),
    )
    coeffs_two = sums_two / count
    fem_twice = fem_once - combine(coeffs_two, fem_flat)
    bem_twice = bem_once - combine(coeffs_two, bem_flat)
    cross_term = jnp.dot(coeffs_two.T, coeffs_two, precision=HIGHEST)
    weighted = jnp.dot(
        coeffs_two.T, jnp.dot(basis_gram / count, coeffs_two, precision=HIGHEST), precision=HIGHEST
    )
    gram_matrix = gram_once / count - 2.0 * cross_term + weighted
    lower_factor = jnp.linalg.cholesky(gram_matrix)
    inverse_lower = jax.scipy.linalg.solve_triangular(
        lower_factor, jnp.eye(rhs_count, dtype=jnp.float32), lower=True
    )
    next_fem = combine(inverse_lower.T, fem_twice)
    next_bem = combine(inverse_lower.T, bem_twice)
    hessenberg = (coeffs_one + coeffs_two).reshape(blocks, rhs_count, rhs_count)
    return (next_fem, next_bem, hessenberg, lower_factor.T)


def solution(mesh):
    return jax.shard_map(
        body,
        mesh=mesh,
        in_specs=(
            P(None, None, None, ("row", "col")),
            P(None, None, None, ("row", "col")),
            P(("row", "col")),
            P(None, ("row", "col")),
            P(None, ("row", "col")),
            P(None, ("row", "col")),
            P(None, "row", "col"),
            P(("row", "col")),
            P(("row", "col")),
        ),
        out_specs=(P(None, None, ("row", "col")), P(None, None, ("row", "col")), P(), P()),
        check_vma=False,
    )
```

profile of v0, /device:TPU:0, one launch (start us, length us, event | category | flops | bytes accessed | tf_op | source)
XLA Modules:
  0.0 561.0 jit_solution(733801144870429433)
XLA Ops:
  10.6 2.1 gather_fusion
  13.6 5.6 collective-permute-start
  21.9 2.1 reshape.200
  24.0 7.0 %all-to-all-start = ((f32[32,1,1024]{2,1,0:T(1,128)}), f32[32,1,1024]{2,1,0:T(1,128)}, u32[]{:S(2)}, u32[]{:S(2)}) async-start(f32[32,1,1024]{2,1,0:T(1,128)} %reshape.200), calls=%async_computation | async-start | bytes 262144 | tf_op jit(solution)/shard_map/all_to_all | solution.py:117
  31.1 14.3 %all_gather.3 = bf16[16,2,2048]{2,0,1:T(8,128)(2,1)S(1)} all-gather(bf16[16,2,512]{2,0,1:T(8,128)(2,1)S(1)} %bitcast.216), channel_id=1, replica_groups=mesh['row'=4,'col'=8] {'row'}, dimensions={2}, use_global_device_ids=true | all-gather | bytes 163840 | tf_op jit(solution)/shard_map/all_gather | solution.py:71
  45.4 15.5 %fusion = f32[16,2,2,4096]{3,0,2,1:T(8,128)S(1)} fusion(bf16[2,4096,2048]{2,1,0:T(8,128)(2,1)} %param.15, bf16[16,2,2048]{2,0,1:T(8,128)(2,1)S(1)} %all_gather.3), kind=kOutput, calls=%fused_computation.4 | convolution fusion | flops 1073741824 | bytes 34734080 | tf_op jit(solution)/shard_map/dot_general | solution.py:73
  63.2 7.5 %gather_fusion.2 = f32[1024,16,2]{1,2,0:T(2,128)} fusion(f32[16,2,2048]{0,1,2:T(2,128)S(1)} %bitcast.190, s32[1024]{0:T(1024)S(1)} %get-tuple-element.32), kind=kCustom, calls=%fused_computation.2 | custom fusion | bytes 266240 | tf_op jit(solution)/shard_map/jit(_take)/gather | solution.py:103
  70.7 6.7 %fusion.73 = f32[1024,2,16]{2,1,0:T(2,128)S(1)} fusion(f32[1024]{0:T(1024)S(1)} %get-tuple-element.33, f32[1024,16,2]{1,2,0:T(2,128)} %gather_fusion.2, pred[1024]{0:T(1024)(128)(4,1)S(1)} %get-tuple-element.34), kind=kLoop, calls=%fused_computation.118 | loop fusion | flops 65536 | bytes 267264
  79.2 2.1 reshape.198
  81.9 4.9 all-to-all-start.1
  88.0 2.2 collective-permute-start.2
  90.2 1.5 collective-permute-start.3
  94.2 1.9 reduce.9
  98.5 2.4 reshape.199
  100.8 2.9 multiply_bitcast_fusion.1
  106.8 224.3 %gather_fusion.1 = f32[32768,16,2]{1,2,0:T(2,128)} fusion(f32[16,2,2560]{0,1,2:T(2,128)} %bitcast_dynamic-update-slice_fusion, s32[32768]{0:T(1024)S(1)} %broadcast_clamp_fusion), kind=kCustom, calls=%fused_computation.1 | custom fusion | bytes 8519680 | tf_op jit(solution)/shard_map/jit(_take)/gather | solution.py:65
  331.1 78.8 %multiply_reduce_fusion = f32[2048,16,2]{1,2,0:T(2,128)} fusion(f32[16,2048,16,2]{2,3,1,0:T(2,128)} %bitcast.188, pred[16,2048]{1,0:T(8,128)(4,1)S(1)} %copy-done.10, f32[16,2048]{1,0:T(8,128)S(1)} %copy-done.9), kind=kLoop, calls=%fused_computation.6 | loop fusion | flops 3080192 | bytes 4620288 | tf_op jit(solution)/shard_map/reduce_sum | solution.py:66
  409.9 6.8 %bitcast_add_fusion = f32[16,2,2048]{0,1,2:T(2,128)S(1)} fusion(f32[2048,16,2]{1,2,0:T(2,128)} %multiply_reduce_fusion, f32[2048]{0:T(1024)S(1)} %copy-done.15, f32[1,16,2,2048]{1,2,3,0:T(2,128)S(1)} %copy-done.1), kind=kLoop, calls=%fused_computation.10 | loop fusion | flops 131072 | bytes 794624 | tf_op jit(solution)/shard_map/add | solution.py:66
  416.8 34.0 %scatter_fusion = f32[16,2,2048]{0,1,2:T(2,128)S(1)} fusion(f32[16,2,2048]{0,1,2:T(2,128)S(1)} %bitcast_add_fusion, s32[1024]{0:T(1024)S(1)} %copy-done.14, f32[1024,16,2]{1,2,0:T(2,128)S(1)} %multiply_bitcast_fusion.1), kind=kCustom, calls=%fused_computation.3 | custom fusion | flops 32768 | bytes 397312 | tf_op jit(solution)/shard_map/scatter-add | solution.py:119
  451.7 1.9 copy.134
  454.3 3.1 fusion.12
  457.6 43.5 %psum.28 = f32[32,16]{0,1:T(8,128)S(1)} all-reduce(f32[32,16]{0,1:T(8,128)S(1)} %fusion.17), channel_id=1, replica_groups=mesh['row'=4,'col'=8] {'row','col'}, use_global_device_ids=true, to_apply=%region_3.4 | all-reduce | flops 512 | bytes 4096 | tf_op jit(solution)/shard_map/psum | solution.py:132
  503.5 41.5 %all-reduce = (f32[16,16]{0,1:T(8,128)S(1)}, f32[32,16]{0,1:T(8,128)S(1)}, f32[32,32]{1,0:T(8,128)S(1)}) all-reduce(f32[16,16]{0,1:T(8,128)S(1)} %fusion.18, f32[32,16]{0,1:T(8,128)S(1)} %fusion.16, f32[32,32]{1,0:T(8,128)S(1)} %convolution_add_fusion), channel_id=1, replica_groups=mesh['row'=4,'col'=8] {'row','col'}, use_global_device_ids=true, to_apply=%region_4.5 | all-reduce | flops 1792 | bytes 14336 | tf_op jit(solution)/shard_map/psum | solution.py:136
  547.1 1.5 cholesky.17
  (125 shorter events, 32.4 us)
Async XLA Ops:
  7.2 13.3 %copy-start.6 = (f32[2,16,2,512]{3,2,1,0:T(2,128)S(1)}, f32[2,16,2,512]{3,2,1,0:T(2,128)}, u32[]{:S(2)}) copy-start(f32[2,16,2,512]{3,2,1,0:T(2,128)} %param.10) | copy-start | bytes 393220
  7.2 13.3 %copy-start.16 = (s32[512]{0:T(512)S(1)}, s32[512]{0:T(512)}, u32[]{:S(2)}) copy-start(s32[512]{0:T(512)} %param.17) | copy-start | bytes 6148
  10.6 66.8 %copy-start = (f32[1,16,2,2048]{1,2,3,0:T(2,128)}, f32[1,16,2,2048]{1,2,3,0:T(2,128)S(1)}, u32[]{:S(2)}) copy-start(f32[1,16,2,2048]{1,2,3,0:T(2,128)S(1)} %copy.161) | copy-start | bytes 786436
  13.6 73.5 %collective-permute-start = (f32[1,1,32,512]{3,2,1,0:T(8,128)}, f32[1,1,32,512]{3,2,1,0:T(8,128)}, u32[]{:S(2)}, u32[]{:S(2)}) collective-permute-start(f32[1,1,32,512]{3,2,1,0:T(8,128)} %broadcast_select_fusion), channel_id=1, source_target_pairs={{0,8},{8,16},{16,24},{1,9},{9,17},{17,25},{2,10},{10,18},{18,26},{... | collective-permute-start | bytes 196616 | tf_op jit(solution)/shard_map/ppermute | solution.py:17
  19.2 67.9 %collective-permute-start.1 = (f32[1,1,32,512]{3,2,1,0:T(8,128)}, f32[1,1,32,512]{3,2,1,0:T(8,128)}, u32[]{:S(2)}, u32[]{:S(2)}) collective-permute-start(f32[1,1,32,512]{3,2,1,0:T(8,128)} %broadcast_select_fusion), channel_id=1, source_target_pairs={{8,0},{16,8},{24,16},{9,1},{17,9},{25,17},{10,2},{18,10},{26,18},{... | collective-permute-start | bytes 196616 | tf_op jit(solution)/shard_map/ppermute | solution.py:19
  24.0 57.9 %all-to-all-start = ((f32[32,1,1024]{2,1,0:T(1,128)}), f32[32,1,1024]{2,1,0:T(1,128)}, u32[]{:S(2)}, u32[]{:S(2)}) async-start(f32[32,1,1024]{2,1,0:T(1,128)} %reshape.200), calls=%async_computation | async-start | bytes 262144 | tf_op jit(solution)/shard_map/all_to_all | solution.py:117
  31.1 423.2 %reduce-scatter.2.cloned.1.call-start = ((), (), s32[]{:S(2)}) async-start(), calls=%async_computation.3 | async-start | bytes 589824 | tf_op jit(solution)/shard_map/reduce_scatter | solution.py:80
  60.9 1.6 copy-start.13
  62.6 16.3 %copy-start.11 = (f32[1024]{0:T(1024)}, f32[1024]{0:T(1024)S(1)}, u32[]{:S(2)}) copy-start(f32[1024]{0:T(1024)S(1)} %get-tuple-element.33) | copy-start | bytes 12292
  77.4 1.4 copy-start.4
  79.2 18.3 %copy-start.2 = (f32[4,8,2,2048]{3,1,2,0:T(8,128)}, f32[4,8,2,2048]{3,1,2,0:T(8,128)S(1)}, u32[]{:S(2)}) copy-start(f32[4,8,2,2048]{3,1,2,0:T(8,128)S(1)} %copy.178) | copy-start | bytes 1572868
  81.3 19.5 %copy-start.12 = (f32[1024]{0:T(1024)S(1)}, f32[1024]{0:T(1024)}, u32[]{:S(2)}) copy-start(f32[1024]{0:T(1024)} %copy-done.11) | copy-start | bytes 12292
  81.9 15.6 %all-to-all-start.1 = ((f32[32,1,1024]{2,1,0:T(1,128)}), f32[32,1,1024]{2,1,0:T(1,128)S(1)}, u32[]{:S(2)}, u32[]{:S(2)}) async-start(f32[32,1,1024]{2,1,0:T(1,128)} %reshape.198), calls=%async_computation.2 | async-start | bytes 262144 | tf_op jit(solution)/shard_map/all_to_all | solution.py:116
  88.0 15.8 %collective-permute-start.2 = (f32[3,1,32,512]{3,2,1,0:T(8,128)S(1)}, f32[3,1,32,512]{3,2,1,0:T(8,128)S(1)}, u32[]{:S(2)}, u32[]{:S(2)}) collective-permute-start(f32[3,1,32,512]{3,2,1,0:T(8,128)S(1)} %pad_maximum_fusion.1), channel_id=1, source_target_pairs={{0,1},{1,2},{2,3},{3,4},{4,5},{5,6},{6,7},{8,9},{9,10},{10,11},{11... | collective-permute-start | bytes 589832 | tf_op jit(solution)/shard_map/ppermute | solution.py:17
  90.2 13.8 %collective-permute-start.3 = (f32[3,1,32,512]{3,2,1,0:T(8,128)S(1)}, f32[3,1,32,512]{3,2,1,0:T(8,128)S(1)}, u32[]{:S(2)}, u32[]{:S(2)}) collective-permute-start(f32[3,1,32,512]{3,2,1,0:T(8,128)S(1)} %pad_maximum_fusion.1), channel_id=1, source_target_pairs={{1,0},{2,1},{3,2},{4,3},{5,4},{6,5},{7,6},{9,8},{10,9},{11,10},{12... | collective-permute-start | bytes 589832 | tf_op jit(solution)/shard_map/ppermute | solution.py:19
  106.8 224.3 %copy-start.9 = (f32[16,2048]{1,0:T(8,128)S(1)}, f32[16,2048]{1,0:T(8,128)}, u32[]{:S(2)}) copy-start(f32[16,2048]{1,0:T(8,128)} %param.12) | copy-start | bytes 393220
  106.8 224.3 %copy-start.10 = (pred[16,2048]{1,0:T(8,128)(4,1)S(1)}, pred[16,2048]{1,0:T(8,128)(4,1)}, u32[]{:S(2)}) copy-start(pred[16,2048]{1,0:T(8,128)(4,1)} %compare_and_fusion) | copy-start | bytes 98308
  331.1 78.8 %copy-start.1 = (f32[1,16,2,2048]{1,2,3,0:T(2,128)S(1)}, f32[1,16,2,2048]{1,2,3,0:T(2,128)}, u32[]{:S(2)}) copy-start(f32[1,16,2,2048]{1,2,3,0:T(2,128)} %copy-done) | copy-start | bytes 786436
  331.1 78.8 %copy-start.15 = (f32[2048]{0:T(1024)S(1)}, f32[2048]{0:T(1024)}, u32[]{:S(2)}) copy-start(f32[2048]{0:T(1024)} %param.11) | copy-start | bytes 24580
  409.9 6.9 %copy-start.14 = (s32[1024]{0:T(1024)S(1)}, s32[1024]{0:T(1024)}, u32[]{:S(2)}) copy-start(s32[1024]{0:T(1024)} %get-tuple-element.31) | copy-start | bytes 12292
  450.8 3.0 copy-start.3
  450.8 3.5 copy-start.17
  453.6 47.7 %copy-start.5 = (f32[2,16,2,2048]{3,2,1,0:T(2,128)S(1)}, f32[2,16,2,2048]{3,2,1,0:T(2,128)}, u32[]{:S(2)}) copy-start(f32[2,16,2,2048]{3,2,1,0:T(2,128)} %param.9) | copy-start | bytes 1572868
  453.6 47.7 %copy-start.7 = (f32[16,2,2048]{2,0,1:T(8,128)S(1)}, f32[16,2,2048]{2,0,1:T(8,128)}, u32[]{:S(2)}) copy-start(f32[16,2,2048]{2,0,1:T(8,128)} %copy.134) | copy-start | bytes 786436
  (1 other events, 0.9 us)
Sparse Core Ops, SparseCore 0:
  62.0 34.3 reduce-scatter.1
where the time goes:
time: 562 us; the launch traced here: 561 us
  local copies, waits for them, and re-layouts  258 us (46%)
  other arithmetic  141 us (25%)
  blocking collectives  99.3 us (18%)
  matrix products  25.3 us (5%)
  starting transfers between devices  22.5 us (4%)
  between operations  14.7 us (3%)
    gather x1, local copies, waits for them, and re-layouts, fem_product(): gathered = jnp.take(extended, fem_columns, axis=2)  224 us
    reduce_sum x1, other arithmetic, fem_product(): return fem_diagonal * vectors + jnp.sum(fem_values * gathered, axis=2)  78.8 us
    psum x1, blocking collectives, body(): lax.psum(dotted(fem_flat, fem_image) + dotted(bem_flat, bem_image), ('row...  43.5 us
    psum x1, blocking collectives, body(): lax.psum((dotted(fem_flat, fem_once) + dotted(bem_flat, bem_once), dotted...  41.5 us
    scatter-add x1, other arithmetic, body(): fem_image = fem_image.at[:, :, clipped].add(answers * mask_row)  34 us
    unnamed x58, local copies, waits for them, and re-layouts  16.5 us
    dot_general x1, matrix products, bem_product(): lax.dot_general(flat_part, bem_matrix, (((1,), (2,)), ((), ())), preferre...  15.5 us
    all_gather x1, blocking collectives, bem_product(): portion = lax.all_gather(rounded, 'row', axis=2, tiled=True)  14.3 us
  transfers between devices with their start and end apart: 7, of which 0 were waited for; matrix products, arithmetic and copies ran while one was open for 72% of the time, Pallas kernels for 0%

commit v1 on v0

v1 whole, which is shorter than its diff:
```python
import functools

import jax
import jax.numpy as jnp
from jax import lax
from jax.experimental import pallas as pl
from jax.experimental.pallas import tpu as pltpu
from jax.sharding import PartitionSpec as P

F32 = jnp.float32
BF16 = jnp.bfloat16
I32 = jnp.int32
HIGHEST = lax.Precision.HIGHEST
LANES = 128
SUB = 8
NT = (((1,), (1,)), ((), ()))
NN = (((1,), (0,)), ((), ()))
ANY = pl.BlockSpec(memory_space=pl.ANY)


def rows8(block, k):
    return jnp.broadcast_to(block[k : k + 1], (SUB, LANES))


def lookup(load, index, chunks, groups, first=0):
    lane = index & (LANES - 1)
    chunk = index >> 7
    picked = [jnp.zeros((SUB, LANES), F32) for _ in range(groups)]
    for c in range(first, chunks):
        here = chunk == c
        for g in range(groups):
            taken = jnp.take_along_axis(load(g, c), lane, axis=1)
            picked[g] = jnp.where(here, taken, picked[g])
    return picked


def chunk_of(ref, base=0):
    def load(g, c):
        return ref[base + SUB * g : base + SUB * (g + 1), LANES * c : LANES * (c + 1)]

    return load


def across(index_row):
    return jnp.transpose(jnp.broadcast_to(index_row, (LANES, LANES)))


def inverse(columns, count, wanted):
    best = jnp.full((SUB, LANES), -1, I32)
    sub = lax.broadcasted_iota(I32, (SUB, LANES), 0)
    for r in range(count // SUB):
        best = jnp.where(columns(r) == wanted, sub + SUB * r, best)
    top = jnp.max(best.astype(F32), axis=0, keepdims=True).astype(I32)
    return jnp.broadcast_to(top, (SUB, LANES))


def lane_ids():
    return lax.broadcasted_iota(I32, (SUB, LANES), 1)


def start_all(copies):
    for copy in copies:
        copy.start()
    return copies


def wait_all(copies):
    for copy in copies:
        copy.wait()


def send_kernel(sizes, fem_hbm, bem_hbm, halo_ref, trace_ref, slot_ref, u_ref, out_ref, mail_ref, phi_ref, bem_ref, col_ref, sem):
    blocks, rhs, nf, nb, width, slots, fold = sizes
    groups = 2 * rhs // SUB
    copies = start_all(
        [pltpu.make_async_copy(bem_hbm.at[blocks - 1, :, p, :], bem_ref.at[pl.ds(rhs * p, rhs), :], sem.at[p]) for p in range(2)]
        + [pltpu.make_async_copy(fem_hbm.at[blocks - 1, :, p, :], u_ref.at[pl.ds(rhs * p, rhs), :], sem.at[2 + p]) for p in range(2)]
    )
    for c in range(nb // LANES):
        col_ref[LANES * c : LANES * (c + 1), :] = across(slot_ref[c : c + 1, :])
    owners = []
    for t in range(slots // LANES):
        owners.append(
            inverse(lambda r: col_ref[SUB * r : SUB * (r + 1), :], nb, lane_ids() + LANES * t)
        )
    wait_all(copies)
    phi_ref[...] = bem_ref[...].astype(BF16)
    for d in range(4):
        for t in range(width // LANES):
            index = rows8(halo_ref[:, LANES * t : LANES * (t + 1)], d)
            for g, got in enumerate(lookup(chunk_of(u_ref), index, nf // LANES, groups)):
                out_ref[d, SUB * g : SUB * (g + 1), LANES * t : LANES * (t + 1)] = got
    for t in range(slots // LANES):
        index = rows8(trace_ref[...], t)
        ask = lookup(chunk_of(u_ref), jnp.where(index >= 0, index, -LANES), nf // LANES, groups)
        give = lookup(chunk_of(bem_ref), owners[t], nb // LANES, groups)
        if fold:
            lane_block = lane_ids() // (LANES // fold)
            for e in range(fold):
                for h, parts in enumerate((ask, give)):
                    for b in range(groups // fold):
                        sheet = None
                        for q in range(fold):
                            moved = parts[b * fold + q]
                            shift = ((q - e) * (LANES // fold)) % LANES
                            moved = pltpu.roll(moved, shift, 1) if shift else moved
                            sheet = moved if sheet is None else jnp.where(lane_block == q, moved, sheet)
                        at = SUB * (h * (groups // fold) + b)
                        mail_ref[t * fold + e, at : at + SUB, :] = sheet
        else:
            for g in range(groups):
                mail_ref[SUB * g : SUB * (g + 1), LANES * t : LANES * (t + 1)] = ask[g]
                mail_ref[2 * rhs + SUB * g : 2 * rhs + SUB * (g + 1), LANES * t : LANES * (t + 1)] = give[g]


def fem_tile(t, sizes, span, u_ref, halo_refs, col_ref, val_ref, start):
    rhs, nf, width, nz = sizes
    groups = 2 * rhs // SUB
    first, last = span
    inner = nf // LANES
    per = width // LANES
    at = pl.ds(pl.multiple_of(t * LANES, LANES), LANES)

    def load(g, c):
        if c < inner:
            return u_ref[SUB * g : SUB * (g + 1), LANES * c : LANES * (c + 1)]
        d, w = divmod(c - inner, per)
        return halo_refs[d][SUB * g : SUB * (g + 1), LANES * w : LANES * (w + 1)]

    sums = start(at)
    for kk in range(nz // SUB):
        cols = col_ref[SUB * kk : SUB * (kk + 1), at]
        vals = val_ref[SUB * kk : SUB * (kk + 1), at]
        for k in range(SUB):
            got = lookup(load, rows8(cols, k), last, groups, first)
            weight = rows8(vals, k)
            sums = [s + weight * x for s, x in zip(sums, got)]
    return at, sums


def own_kernel(sizes, tiles, u_ref, col_ref, val_ref, diag_ref, o_ref):
    rhs, nf, _, _ = sizes

    def start(at):
        scale = diag_ref[pl.ds(0, 1), at]
        return [u_ref[SUB * g : SUB * (g + 1), at] * scale for g in range(2 * rhs // SUB)]

    def step(t, carry):
        at, sums = fem_tile(t, sizes, (0, nf // LANES), u_ref, None, col_ref, val_ref, start)
        for g, s in enumerate(sums):
            o_ref[SUB * g : SUB * (g + 1), at] = s
        return carry

    lax.fori_loop(0, tiles, step, 0)


def bem_kernel(sizes, tiles, each, phi_ref, m_ref, u_ref, h0, h1, h2, h3, col_ref, val_ref, diag_ref, part_ref, o_ref, f_ref):
    rhs, nf, width, nz = sizes
    i = pl.program_id(0)
    phi = jnp.concatenate([phi_ref[r] for r in range(phi_ref.shape[0])], axis=1)
    p0 = lax.dot_general(phi, m_ref[0], NT, preferred_element_type=F32)
    p1 = lax.dot_general(phi, m_ref[1], NT, preferred_element_type=F32)
    o_ref[0, 0:rhs] = p0[0:rhs] - p1[rhs:]
    o_ref[0, rhs:] = p1[0:rhs] + p0[rhs:]
    halos = (h0, h1, h2, h3)
    inner = nf // LANES
    outer = inner + 4 * (width // LANES)

    def step(j, carry):
        t = i * each + j

        def own(at):
            return [part_ref[SUB * g : SUB * (g + 1), at] for g in range(2 * rhs // SUB)]

        def fresh(at):
            scale = diag_ref[pl.ds(0, 1), at]
            return [u_ref[SUB * g : SUB * (g + 1), at] * scale for g in range(2 * rhs // SUB)]

        @pl.when(t < tiles)
        def _():
            at, sums = fem_tile(t, sizes, (inner, outer), u_ref, halos, col_ref, val_ref, own)
            for g, s in enumerate(sums):
                f_ref[SUB * g : SUB * (g + 1), at] = s

        @pl.when(t >= tiles)
        def _():
            at, sums = fem_tile(t, sizes, (0, outer), u_ref, halos, col_ref, val_ref, fresh)
            for g, s in enumerate(sums):
                f_ref[SUB * g : SUB * (g + 1), at] = s

        return carry

    lax.fori_loop(0, each, step, 0)


def split(x):
    high = x.astype(BF16)
    return high, (x - high.astype(F32)).astype(BF16)


def products(q, w):
    rows = jnp.concatenate([q, w], axis=0)
    pad = jnp.zeros((LANES - rows.shape[0], rows.shape[1]), F32)
    high, low = split(rows)
    high_all, low_all = split(jnp.concatenate([rows, pad], axis=0))
    total = lax.dot_general(high, high_all, NT, preferred_element_type=F32)
    total += lax.dot_general(high, low_all, NT, preferred_element_type=F32)
    total += lax.dot_general(low, high_all, NT, preferred_element_type=F32)
    return total


def trace_kernel(sizes, fem_hbm, f_ref, mail_ref, trace_ref, slot_ref, w_ref, add_ref, z_ref, col_ref, got_ref, q_ref, sem):
    blocks, rhs, nf, nb, width, slots, fold = sizes
    groups = 2 * rhs // SUB
    copies = start_all(
        [
            pltpu.make_async_copy(fem_hbm.at[b, :, p, :], q_ref.at[p, pl.ds(rhs * b, rhs), :], sem.at[2 * b + p])
            for b in range(blocks)
            for p in range(2)
        ]
    )
    for c in range(slots // LANES):
        col_ref[LANES * c : LANES * (c + 1), :] = across(trace_ref[c : c + 1, :])
    if fold:
        lane_block = lane_ids() // (LANES // fold)
        for t in range(slots // LANES):
            for h in range(2):
                for g in range(groups):
                    b, q = divmod(g, fold)
                    at = SUB * (h * (groups // fold) + b)
                    sheet = None
                    for e in range(fold):
                        moved = mail_ref[t * fold + e, at : at + SUB, :]
                        shift = ((e - q) * (LANES // fold)) % LANES
                        moved = pltpu.roll(moved, shift, 1) if shift else moved
                        sheet = moved if sheet is None else jnp.where(lane_block == e, moved, sheet)
                    row = 2 * rhs * h + SUB * g
                    got_ref[row : row + SUB, LANES * t : LANES * (t + 1)] = sheet
    else:
        got_ref[...] = mail_ref[...]
    for t in range(nb // LANES):
        index = rows8(slot_ref[...], t)
        for g, got in enumerate(lookup(chunk_of(got_ref), index, slots // LANES, groups)):
            add_ref[SUB * g : SUB * (g + 1), LANES * t : LANES * (t + 1)] = got

    def step(t, carry):
        at = pl.ds(pl.multiple_of(t * LANES, LANES), LANES)
        index = inverse(lambda r: col_ref[SUB * r : SUB * (r + 1), :], slots, lane_ids() + LANES * t)
        for g, got in enumerate(lookup(chunk_of(got_ref, 2 * rhs), index, slots // LANES, groups)):
            w_ref[SUB * g : SUB * (g + 1), at] = f_ref[SUB * g : SUB * (g + 1), at] + got
        return carry

    lax.fori_loop(0, nf // LANES, step, 0)
    wait_all(copies)
    z_ref[...] = products(q_ref[0], w_ref[0:rhs]) + products(q_ref[1], w_ref[rhs:])


def sums_kernel(sizes, bem_hbm, parts_ref, add_ref, z_ref, w_ref, o_ref, q_ref, sem):
    blocks, rhs = sizes
    copies = start_all(
        [
            pltpu.make_async_copy(bem_hbm.at[b, :, p, :], q_ref.at[p, pl.ds(rhs * b, rhs), :], sem.at[2 * b + p])
            for b in range(blocks)
            for p in range(2)
        ]
    )
    total = add_ref[...]
    for d in range(parts_ref.shape[0]):
        total = total + parts_ref[d]
    w_ref[...] = total
    wait_all(copies)
    z = z_ref[...] + products(q_ref[0], total[0:rhs]) + products(q_ref[1], total[rhs:])
    basis = blocks * rhs
    lane = lax.broadcasted_iota(I32, (rhs, LANES), 1)
    packed = z[basis:]
    for b in range(blocks):
        shift = LANES - basis * (blocks - b)
        packed = packed + pltpu.roll(jnp.where(lane < basis, z[rhs * b : rhs * (b + 1)], 0.0), shift, 1)
    o_ref[...] = packed


def factor(gram, rhs):
    row = lax.broadcasted_iota(I32, (rhs, LANES), 0)
    lane = lax.broadcasted_iota(I32, (rhs, LANES), 1)
    work = jnp.where(lane == row + rhs, 1.0, gram)
    done = jnp.zeros((rhs, LANES), F32)
    for k in range(rhs):
        pivot = jnp.broadcast_to(work[k : k + 1, k : k + 1], (1, LANES))
        line = work[k : k + 1, :] / jnp.sqrt(pivot)
        scale = line[:, k : k + 1]
        column = jnp.sum(jnp.where(lane == k, work, 0.0), axis=1, keepdims=True)
        done = jnp.where(row == k, line, done)
        work = work - (column / scale) * line
    return done


def last_kernel(sizes, fem_hbm, bem_hbm, all_ref, wf_ref, wb_ref, nf_hbm, nb_hbm, h_ref, r_ref, q_ref, b_ref, of_ref, ob_ref, sem):
    blocks, rhs, count = sizes
    basis = blocks * rhs
    copies = start_all(
        [
            pltpu.make_async_copy(hbm.at[b, :, p, :], ref.at[p, pl.ds(rhs * b, rhs), :], sem.at[s, 2 * b + p])
            for s, (hbm, ref) in enumerate(((fem_hbm, q_ref), (bem_hbm, b_ref)))
            for b in range(blocks)
            for p in range(2)
        ]
    )
    total = all_ref[0]
    for d in range(1, all_ref.shape[0]):
        total = total + all_ref[d]
    total = total / count
    c1 = total[:, 0:basis]
    g = jnp.concatenate(
        [pltpu.roll(total, basis * (blocks - b), 1)[:, 0:basis] for b in range(blocks)], axis=0
    )
    lane = lax.broadcasted_iota(I32, (rhs, LANES), 1)
    own = jnp.where(lane < rhs, pltpu.roll(total, LANES - basis, 1), 0.0)

    def dot(x, y, dims):
        return lax.dot_general(x, y, dims, precision=HIGHEST, preferred_element_type=F32)

    c2 = c1 - dot(c1, g, NN)
    h = c1 + c2
    rest = 2.0 * c1 - dot(h, g, NN)
    rest_pad = jnp.concatenate([rest, jnp.zeros((LANES - rhs, basis), F32)], axis=0)
    gram = own - dot(h, rest_pad, NT)
    gram = jnp.where(lane < rhs, gram, 0.0)
    done = factor(gram, rhs)
    below = done[:, rhs : 2 * rhs]
    r_ref[...] = done[:, 0:rhs]
    eye = (
        lax.broadcasted_iota(I32, (basis, basis), 0) == lax.broadcasted_iota(I32, (basis, basis), 1)
    ).astype(F32)
    h_ref[...] = dot(eye, h, NT)
    mix = jnp.concatenate([-dot(below, h, NN), below], axis=1)
    mix_high, mix_low = split(mix)

    def finish(q, w, p):
        high, low = split(jnp.concatenate([q[p], w[rhs * p : rhs * (p + 1)]], axis=0))
        out = lax.dot_general(mix_high, high, NN, preferred_element_type=F32)
        out += lax.dot_general(mix_high, low, NN, preferred_element_type=F32)
        out += lax.dot_general(mix_low, high, NN, preferred_element_type=F32)
        return out

    wait_all(copies)
    copies = []
    for s, (q, w, o, hbm) in enumerate(((q_ref, wf_ref, of_ref, nf_hbm), (b_ref, wb_ref, ob_ref, nb_hbm))):
        for p in range(2):
            o[p] = finish(q, w, p)
            copies += start_all([pltpu.make_async_copy(o.at[p], hbm.at[:, p, :], sem.at[s, p])])
    wait_all(copies)


def shape(*dims, dtype=F32):
    return jax.ShapeDtypeStruct(dims, dtype)


def neighbours(axis, step):
    n = lax.axis_size(axis)
    return [(i, i + step) for i in range(n) if 0 <= i + step < n]


def spread(x, axes):
    n = lax.axis_size(axes)
    return lax.all_to_all(jnp.broadcast_to(x[None], (n,) + x.shape), axes, 0, 0, tiled=True)


def body(fem_basis, bem_basis, fem_diagonal, fem_values, fem_columns, halo_rows, bem_matrix, trace_rows, bem_slot):
    blocks, rhs, _, nf = fem_basis.shape
    nb = bem_basis.shape[3]
    nz = fem_values.shape[0]
    width = halo_rows.shape[1]
    slots = trace_rows.shape[0]
    n_row, n_col = lax.axis_size("row"), lax.axis_size("col")
    devices = n_row * n_col
    both = ("row", "col")
    groups = 2 * rhs // SUB
    room = slots // devices
    fold = LANES // room
    if LANES % room or groups % fold:
        fold = 0
    mail_shape = (devices, 4 * rhs // fold, LANES) if fold else (4 * rhs, slots)
    traces = trace_rows.reshape(slots // LANES, LANES)
    owned = bem_slot.reshape(nb // LANES, LANES)
    diagonal = fem_diagonal.reshape(1, nf)
    sizes = (blocks, rhs, nf, nb, width, slots, fold)

    vmem = pl.BlockSpec(memory_space=pltpu.VMEM)
    u, out, mail, phi = pl.pallas_call(
        functools.partial(send_kernel, sizes),
        in_specs=[ANY, ANY, vmem, vmem, vmem],
        out_specs=[vmem] * 4,
        out_shape=[shape(2 * rhs, nf), shape(4, 2 * rhs, width), shape(*mail_shape), shape(2 * rhs, nb, dtype=BF16)],
        scratch_shapes=[pltpu.VMEM((2 * rhs, nb), F32), pltpu.VMEM((nb, LANES), I32), pltpu.SemaphoreType.DMA((4,))],
        name="send",
    )(fem_basis, bem_basis, halo_rows, traces, owned)

    phi_all = spread(phi, "row")
    halos = [
        lax.ppermute(out[0], "col", neighbours("col", 1)),
        lax.ppermute(out[1], "col", neighbours("col", -1)),
        lax.ppermute(out[2], "row", neighbours("row", 1)),
        lax.ppermute(out[3], "row", neighbours("row", -1)),
    ]
    if fold:
        mail = lax.all_to_all(mail, both, 0, 0, tiled=True)
    else:
        mail = lax.all_to_all(mail, both, 1, 1, tiled=True)

    fem_sizes = (rhs, nf, width, nz)
    tiles = nf // LANES
    early = tiles // 2
    own = pl.pallas_call(
        functools.partial(own_kernel, fem_sizes, early),
        in_specs=[vmem] * 4,
        out_specs=vmem,
        out_shape=shape(2 * rhs, nf),
        name="own",
    )(u, fem_columns, fem_values, diagonal)

    k_len = bem_matrix.shape[2]
    full = lambda *dims: pl.BlockSpec(dims, lambda i: (0,) * len(dims))
    partial, fem_part = pl.pallas_call(
        functools.partial(bem_kernel, fem_sizes, early, tiles // n_col),
        grid=(n_col,),
        in_specs=[
            full(n_row, 2 * rhs, nb),
            pl.BlockSpec((2, nb, k_len), lambda i: (0, i, 0)),
            full(2 * rhs, nf),
        ]
        + [full(2 * rhs, width)] * 4
        + [full(nz, nf), full(nz, nf), full(1, nf), full(2 * rhs, nf)],
        out_specs=[pl.BlockSpec((1, 2 * rhs, nb), lambda i: (i, 0, 0)), full(2 * rhs, nf)],
        out_shape=[shape(n_col, 2 * rhs, nb), shape(2 * rhs, nf)],
        name="bem",
    )(phi_all, bem_matrix, u, *halos, fem_columns, fem_values, diagonal, own)

    parts = lax.all_to_all(partial, "col", 0, 0, tiled=True)

    basis = blocks * rhs
    w_fem, add, z_fem = pl.pallas_call(
        functools.partial(trace_kernel, sizes),
        in_specs=[ANY] + [vmem] * 4,
        out_specs=[vmem] * 3,
        out_shape=[shape(2 * rhs, nf), shape(2 * rhs, nb), shape(basis + rhs, LANES)],
        scratch_shapes=[
            pltpu.VMEM((slots, LANES), I32),
            pltpu.VMEM((4 * rhs, slots), F32),
            pltpu.VMEM((2, basis, nf), F32),
            pltpu.SemaphoreType.DMA((2 * blocks,)),
        ],
        name="trace",
    )(fem_basis, fem_part, mail, traces, owned)

    w_bem, local = pl.pallas_call(
        functools.partial(sums_kernel, (blocks, rhs)),
        in_specs=[ANY] + [vmem] * 3,
        out_specs=[vmem] * 2,
        out_shape=[shape(2 * rhs, nb), shape(rhs, LANES)],
        scratch_shapes=[pltpu.VMEM((2, basis, nb), F32), pltpu.SemaphoreType.DMA((2 * blocks,))],
        name="sums",
    )(bem_basis, parts, add, z_fem)

    everyone = spread(local, both)

    next_fem, next_bem, h, r_factor = pl.pallas_call(
        functools.partial(last_kernel, (blocks, rhs, 2.0 * devices * (nf + nb))),
        in_specs=[ANY, ANY] + [vmem] * 3,
        out_specs=[ANY, ANY, vmem, vmem],
        out_shape=[shape(rhs, 2, nf), shape(rhs, 2, nb), shape(basis, rhs), shape(rhs, rhs)],
        scratch_shapes=[
            pltpu.VMEM((2, basis, nf), F32),
            pltpu.VMEM((2, basis, nb), F32),
            pltpu.VMEM((2, rhs, nf), F32),
            pltpu.VMEM((2, rhs, nb), F32),
            pltpu.SemaphoreType.DMA((2, 2 * blocks)),
        ],
        name="last",
    )(fem_basis, bem_basis, everyone, w_fem, w_bem)
    return (next_fem, next_bem, h.reshape(blocks, rhs, rhs), r_factor)


def solution(mesh):
    return jax.shard_map(
        body,
        mesh=mesh,
        in_specs=(
            P(None, None, None, ("row", "col")),
            P(None, None, None, ("row", "col")),
            P(("row", "col")),
            P(None, ("row", "col")),
            P(None, ("row", "col")),
            P(None, ("row", "col")),
            P(None, "row", "col"),
            P(("row", "col")),
            P(("row", "col")),
        ),
        out_specs=(P(None, None, ("row", "col")), P(None, None, ("row", "col")), P(), P()),
        check_vma=False,
    )
```

time: 562 us -> 114 us (0.20)
  local copies, waits for them, and re-layouts: 258 us -> 4.27 us
  other arithmetic: 141 us -> 0 us
  blocking collectives: 99.3 us -> 25.9 us
  Pallas kernels: 0 us -> 60.3 us
  matrix products: 25.3 us -> 0 us
  between operations: 14.7 us -> 0.76 us
    gather x5 -> x0, local copies, waits for them, and re-layouts: 234 us -> none  [the longest x1 224 us: fem_product(): gathered = jnp.take(extended, fem_columns, axis=2)]
    psum x2 -> x0, blocking collectives: 85 us -> none  [the longest x1 43.5 us: body(): lax.psum(dotted(fem_flat, fem_image) + dotted(bem_flat, bem_image), ('row...]
    reduce_sum x1 -> x0, other arithmetic: 78.8 us -> none  [fem_product(): return fem_diagonal * vectors + jnp.sum(fem_values * gathered, axis=2)]
    pallas_call x0 -> x6, Pallas kernels: none -> 60.3 us  [the longest x1 29.4 us: body(): pl.pallas_call(functools.partial(bem_kernel, fem_sizes, early, tiles // n...]
    scatter-add x1 -> x0, other arithmetic: 34 us -> none  [body(): fem_image = fem_image.at[:, :, clipped].add(answers * mask_row)]
    all_to_all x0 -> x2, blocking collectives: none -> 25.9 us  [spread(): lax.all_to_all(jnp.broadcast_to(x[None], (n,) + x.shape), axes, 0, 0, til...]
    dot_general x20 -> x0, matrix products: 25.1 us -> none  [the longest x1 15.5 us: bem_product(): lax.dot_general(flat_part, bem_matrix, (((1,), (2,)), ((), ())), preferre...]
    unnamed x58 -> x12, local copies, waits for them, and re-layouts: 16.5 us -> 2 us
  transfers between devices with their start and end apart: 7 -> 6, of which waited for: 0 -> 1; matrix products, arithmetic and copies ran while one was open for 72% -> 1% of each run, Pallas kernels for 0% -> 41%
where the time goes in v1:
time: 114 us; the launch traced here: 113 us
  Pallas kernels  60.3 us (53%)
  blocking collectives  25.9 us (23%)
  starting transfers between devices  18.2 us (16%)
  local copies, waits for them, and re-layouts  4.27 us (4%)
  waiting for transfers between devices  3.83 us (3%)
    pallas_call x1, Pallas kernels, body(): pl.pallas_call(functools.partial(bem_kernel, fem_sizes, early, tiles // n...  29.4 us
    all_to_all x2, blocking collectives, spread(): lax.all_to_all(jnp.broadcast_to(x[None], (n,) + x.shape), axes, 0, 0, til...  25.9 us
    pallas_call x1, Pallas kernels, body(): pl.pallas_call(functools.partial(own_kernel, fem_sizes, early), in_specs=...  11.4 us
    pallas_call x1, Pallas kernels, body(): pl.pallas_call(functools.partial(last_kernel, (blocks, rhs, 2.0 * devices...  6.5 us
    pallas_call x1, Pallas kernels, body(): pl.pallas_call(functools.partial(trace_kernel, sizes), in_specs=[ANY] + [...  5.88 us
    ppermute x1, starting transfers between devices, body(): lax.ppermute(out[2], 'row', neighbours('row', 1))  4.55 us
    all_to_all x1, starting transfers between devices, body(): parts = lax.all_to_all(partial, 'col', 0, 0, tiled=True)  4.36 us
    pallas_call x1, Pallas kernels, body(): pl.pallas_call(functools.partial(send_kernel, sizes), in_specs=[ANY, ANY,...  4.26 us
  transfers between devices with their start and end apart: 6, of which 1 were waited for; matrix products, arithmetic and copies ran while one was open for 1% of the time, Pallas kernels for 41%

profile of v1, /device:TPU:0, one launch (start us, length us, event | category | flops | bytes accessed | tf_op | source)
XLA Modules:
  0.0 113.3 jit_solution(8185799227714888489)
XLA Ops:
  0.6 4.3 %send.1 = (f32[32,2048]{1,0:T(8,128)}, f32[4,32,128]{2,1,0:T(8,128)}, f32[32,16,128]{2,1,0:T(8,128)}, bf16[32,512]{1,0:T(8,128)(2,1)}) custom-call(f32[2,16,2,2048]{3,2,1,0:T(2,128)} %fem_hbm.5, f32[2,16,2,512]{3,2,1,0:T(2,128)} %bem_hbm.5, s32[4,128]{1,0:T(4,128)} %halo_ref.1, s32[8,128]{1,0:T(8,128)} %bitcast.14, s32[4,128]{1,0:T(4,128)} %bitcast.16), custom_call_target="tpu_custom_call" | custom-call | tf_op jit(solution)/shard_map/send/pallas_call | solution.py:389
  4.9 0.8 broadcast_in_dim.4
  5.7 12.3 %all_to_all.20.phi_ref = bf16[4,32,512]{2,1,0:T(8,128)(2,1)} all-to-all(bf16[4,32,512]{2,1,0:T(8,128)(2,1)S(1)} %broadcast_in_dim.4), channel_id=1, replica_groups=mesh['row'=4,'col'=8] {'row'}, dimensions={0} | all-to-all | bytes 262144 | tf_op jit(solution)/shard_map/all_to_all | solution.py:365
  18.0 3.7 %all-to-all-start.2 = ((f32[32,16,128]{2,1,0:T(8,128)}), f32[32,16,128]{2,1,0:T(8,128)S(1)}, u32[]{:S(2)}, u32[]{:S(2)}) async-start(f32[32,16,128]{2,1,0:T(8,128)} %get-tuple-element.24), calls=%async_computation.2 | async-start | bytes 524288 | tf_op jit(solution)/shard_map/all_to_all | solution.py:406
  21.7 0.8 slice_bitcast_fusion
  22.5 1.3 %collective-permute-start.3 = (f32[32,128]{1,0:T(8,128)S(1)}, f32[32,128]{1,0:T(8,128)S(1)}, u32[]{:S(2)}, u32[]{:S(2)}) collective-permute-start(f32[32,128]{1,0:T(8,128)S(1)} %get-tuple-element.34), channel_id=1, source_target_pairs={{8,0},{16,8},{24,16},{9,1},{17,9},{25,17},{10,2},{18,10},{26,18},{... | collective-permute-start | bytes 49160 | tf_op jit(solution)/shard_map/ppermute | solution.py:403
  23.8 4.5 %collective-permute-start.2 = (f32[32,128]{1,0:T(8,128)S(1)}, f32[32,128]{1,0:T(8,128)S(1)}, u32[]{:S(2)}, u32[]{:S(2)}) collective-permute-start(f32[32,128]{1,0:T(8,128)S(1)} %get-tuple-element.35), channel_id=1, source_target_pairs={{0,8},{8,16},{16,24},{1,9},{9,17},{17,25},{2,10},{10,18},{18,26},{... | collective-permute-start | bytes 49160 | tf_op jit(solution)/shard_map/ppermute | solution.py:402
  28.3 1.3 %collective-permute-start.1 = (f32[32,128]{1,0:T(8,128)S(1)}, f32[32,128]{1,0:T(8,128)S(1)}, u32[]{:S(2)}, u32[]{:S(2)}) collective-permute-start(f32[32,128]{1,0:T(8,128)S(1)} %get-tuple-element.36), channel_id=1, source_target_pairs={{1,0},{2,1},{3,2},{4,3},{5,4},{6,5},{7,6},{9,8},{10,9},{11,10},{12... | collective-permute-start | bytes 49160 | tf_op jit(solution)/shard_map/ppermute | solution.py:401
  29.6 3.0 %collective-permute-start = (f32[32,128]{1,0:T(8,128)S(1)}, f32[32,128]{1,0:T(8,128)S(1)}, u32[]{:S(2)}, u32[]{:S(2)}) collective-permute-start(f32[32,128]{1,0:T(8,128)S(1)} %get-tuple-element.37), channel_id=1, source_target_pairs={{0,1},{1,2},{2,3},{3,4},{4,5},{5,6},{6,7},{8,9},{9,10},{10,11},{11... | collective-permute-start | bytes 49160 | tf_op jit(solution)/shard_map/ppermute | solution.py:400
  32.7 11.4 %own.1.part_ref = f32[32,2048]{1,0:T(8,128)} custom-call(f32[32,2048]{1,0:T(8,128)} %get-tuple-element.20.u_ref, s32[16,2048]{1,0:T(8,128)} %col_ref.3, f32[16,2048]{1,0:T(8,128)} %val_ref.3, f32[1,2048]{1,0:T(1,128)} %bitcast.12), custom_call_target="tpu_custom_call" | custom-call | tf_op jit(solution)/shard_map/own/pallas_call | solution.py:413
  44.1 0.0 copy-start.4
  44.1 0.5 copy-done.2
  44.7 0.0 copy-done.4
  44.7 0.6 copy-done.5
  45.3 29.4 %bem.1 = (f32[8,32,512]{2,1,0:T(8,128)}, f32[32,2048]{1,0:T(8,128)}) custom-call(bf16[4,32,512]{2,1,0:T(8,128)(2,1)} %all_to_all.20.phi_ref, bf16[2,4096,2048]{2,1,0:T(8,128)(2,1)} %m_ref.1, f32[32,2048]{1,0:T(8,128)} %get-tuple-element.20.u_ref, f32[32,128]{1,0:T(8,128)} %copy-done.5, f32[32,128]{1,0:T(8,128)} %copy-done.4, f32[32,128]{1,0:T(8,128)} %copy-done.3, ...), custom_call_target="tpu_custom_call" | custom-call | tf_op jit(solution)/shard_map/bem/pallas_call | solution.py:423
  74.7 0.0 copy-start.1
  74.8 4.4 %all-to-all-start.1 = ((f32[8,32,512]{2,1,0:T(8,128)}), f32[8,32,512]{2,1,0:T(8,128)S(1)}, u32[]{:S(2)}, u32[]{:S(2)}) async-start(f32[8,32,512]{2,1,0:T(8,128)} %get-tuple-element.22), calls=%async_computation.1 | async-start | bytes 1048576 | tf_op jit(solution)/shard_map/all_to_all | solution.py:438
  79.1 5.9 %trace.1 = (f32[32,2048]{1,0:T(8,128)}, f32[32,512]{1,0:T(8,128)}, f32[48,128]{1,0:T(8,128)}) custom-call(f32[2,16,2,2048]{3,2,1,0:T(2,128)} %fem_hbm.5, f32[32,2048]{1,0:T(8,128)} %get-tuple-element.23.f_ref, f32[32,16,128]{2,1,0:T(8,128)} %copy-done.1, s32[8,128]{1,0:T(8,128)} %bitcast.15, s32[4,128]{1,0:T(4,128)} %bitcast.17), custom_call_target="tpu_custom_call" | custom-call | tf_op jit(solution)/shard_map/trace/pallas_call | solution.py:441
  85.0 3.8 %all-to-all-done.1.parts_ref = f32[8,32,512]{2,1,0:T(8,128)S(1)} async-done(((f32[8,32,512]{2,1,0:T(8,128)}), f32[8,32,512]{2,1,0:T(8,128)S(1)}, u32[]{:S(2)}, u32[]{:S(2)}) %all-to-all-start.1) | async-done | bytes 524320 | tf_op jit(solution)/shard_map/all_to_all | solution.py:438
  88.8 0.8 copy-done
  89.6 2.9 %sums.1 = (f32[32,512]{1,0:T(8,128)}, f32[16,128]{1,0:T(8,128)}) custom-call(f32[2,16,2,512]{3,2,1,0:T(2,128)} %bem_hbm.5, f32[8,32,512]{2,1,0:T(8,128)} %copy-done, f32[32,512]{1,0:T(8,128)} %get-tuple-element.25.add_ref, f32[48,128]{1,0:T(8,128)} %get-tuple-element.26.z_ref), custom_call_target="tpu_custom_call" | custom-call | tf_op jit(solution)/shard_map/sums/pallas_call | solution.py:455
  92.5 0.7 broadcast_in_dim.5
  93.2 13.6 %all_to_all.21.all_ref = f32[32,16,128]{2,1,0:T(8,128)} all-to-all(f32[32,16,128]{2,1,0:T(8,128)S(1)} %broadcast_in_dim.5), channel_id=1, replica_groups=mesh['row'=4,'col'=8] {'row','col'}, dimensions={0} | all-to-all | bytes 524288 | tf_op jit(solution)/shard_map/all_to_all | solution.py:365
  106.8 6.5 %last.1 = (f32[16,2,2048]{2,1,0:T(2,128)}, f32[16,2,512]{2,1,0:T(2,128)}, f32[32,16]{1,0:T(8,128)}, f32[16,16]{1,0:T(8,128)}) custom-call(f32[2,16,2,2048]{3,2,1,0:T(2,128)} %fem_hbm.5, f32[2,16,2,512]{3,2,1,0:T(2,128)} %bem_hbm.5, f32[32,16,128]{2,1,0:T(8,128)} %all_to_all.21.all_ref, f32[32,2048]{1,0:T(8,128)} %get-tuple-element.28.wf_ref, ...), custom_call_target="tpu_custom_call" | custom-call | tf_op jit(solution)/shard_map/last/pallas_call | solution.py:466
  (11 shorter events, 0.0 us)
Async XLA Ops:
  18.0 56.7 %all-to-all-start.2 = ((f32[32,16,128]{2,1,0:T(8,128)}), f32[32,16,128]{2,1,0:T(8,128)S(1)}, u32[]{:S(2)}, u32[]{:S(2)}) async-start(f32[32,16,128]{2,1,0:T(8,128)} %get-tuple-element.24), calls=%async_computation.2 | async-start | bytes 524288 | tf_op jit(solution)/shard_map/all_to_all | solution.py:406
  22.5 21.6 %collective-permute-start.3 = (f32[32,128]{1,0:T(8,128)S(1)}, f32[32,128]{1,0:T(8,128)S(1)}, u32[]{:S(2)}, u32[]{:S(2)}) collective-permute-start(f32[32,128]{1,0:T(8,128)S(1)} %get-tuple-element.34), channel_id=1, source_target_pairs={{8,0},{16,8},{24,16},{9,1},{17,9},{25,17},{10,2},{18,10},{26,18},{... | collective-permute-start | bytes 49160 | tf_op jit(solution)/shard_map/ppermute | solution.py:403
  23.8 20.3 %collective-permute-start.2 = (f32[32,128]{1,0:T(8,128)S(1)}, f32[32,128]{1,0:T(8,128)S(1)}, u32[]{:S(2)}, u32[]{:S(2)}) collective-permute-start(f32[32,128]{1,0:T(8,128)S(1)} %get-tuple-element.35), channel_id=1, source_target_pairs={{0,8},{8,16},{16,24},{1,9},{9,17},{17,25},{2,10},{10,18},{18,26},{... | collective-permute-start | bytes 49160 | tf_op jit(solution)/shard_map/ppermute | solution.py:402
  28.3 15.8 %collective-permute-start.1 = (f32[32,128]{1,0:T(8,128)S(1)}, f32[32,128]{1,0:T(8,128)S(1)}, u32[]{:S(2)}, u32[]{:S(2)}) collective-permute-start(f32[32,128]{1,0:T(8,128)S(1)} %get-tuple-element.36), channel_id=1, source_target_pairs={{1,0},{2,1},{3,2},{4,3},{5,4},{6,5},{7,6},{9,8},{10,9},{11,10},{12... | collective-permute-start | bytes 49160 | tf_op jit(solution)/shard_map/ppermute | solution.py:401
  29.6 14.5 %collective-permute-start = (f32[32,128]{1,0:T(8,128)S(1)}, f32[32,128]{1,0:T(8,128)S(1)}, u32[]{:S(2)}, u32[]{:S(2)}) collective-permute-start(f32[32,128]{1,0:T(8,128)S(1)} %get-tuple-element.37), channel_id=1, source_target_pairs={{0,1},{1,2},{2,3},{3,4},{4,5},{5,6},{6,7},{8,9},{9,10},{10,11},{11... | collective-permute-start | bytes 49160 | tf_op jit(solution)/shard_map/ppermute | solution.py:400
  44.1 0.6 copy-start.2
  44.1 0.6 copy-start.3
  44.1 0.6 copy-start.4
  44.7 0.6 copy-start.5
  74.7 4.4 %copy-start.1 = (f32[32,16,128]{2,1,0:T(8,128)}, f32[32,16,128]{2,1,0:T(8,128)S(1)}, u32[]{:S(2)}) copy-start(f32[32,16,128]{2,1,0:T(8,128)S(1)} %all-to-all-done.2.mail_ref) | copy-start | bytes 786436
  74.8 14.1 %all-to-all-start.1 = ((f32[8,32,512]{2,1,0:T(8,128)}), f32[8,32,512]{2,1,0:T(8,128)S(1)}, u32[]{:S(2)}, u32[]{:S(2)}) async-start(f32[8,32,512]{2,1,0:T(8,128)} %get-tuple-element.22), calls=%async_computation.1 | async-start | bytes 1048576 | tf_op jit(solution)/shard_map/all_to_all | solution.py:438
  88.8 0.8 copy-start
